TPU v7x, 32 devices: a whole 2x2x4 slice. The times are simulated.
32 devices in a mesh: dp: 8 (over z, x), tensor: 4 (over y, core).
Axes of the slice: x: 2, y: 2, z: 4, core: 2. Of those that a mesh axis runs over, the one named last changes fastest.
Arguments:
- tokens: bfloat16 [16384, 768], P(('dp', 'tensor')), may hold values from -6 to 6
- w_query: bfloat16 [768, 768], P(None, 'tensor'), may hold values from -0.3125 to 0.3125
- w_key: bfloat16 [768, 768], P(None, 'tensor'), may hold values from -0.3125 to 0.3125
- w_value: bfloat16 [768, 768], P(None, 'tensor'), may hold values from -0.21875 to 0.21875
- b_query: bfloat16 [768], P('tensor'), may hold values from -3 to 3
- b_value: bfloat16 [768], P('tensor'), may hold values from -3 to 3
- w_output: bfloat16 [768, 768], P('tensor'), may hold values from -0.375 to 0.375
- b_output: bfloat16 [768], replicated, may hold values from -3 to 3
- first_gain: bfloat16 [768], replicated, may hold values from 0.5 to 1.5
- first_shift: bfloat16 [768], replicated, may hold values from -3 to 3
- w_up: bfloat16 [768, 3072], P(None, 'tensor'), may hold values from -0.21875 to 0.21875
- b_up: bfloat16 [3072], P('tensor'), may hold values from -3 to 3
- w_down: bfloat16 [3072, 768], P('tensor'), may hold values from -0.15625 to 0.15625
- b_down: bfloat16 [768], replicated, may hold values from -3 to 3
- second_gain: bfloat16 [768], replicated, may hold values from 0.5 to 1.5
- second_shift: bfloat16 [768], replicated, may hold values from -3 to 3
- cotangent: bfloat16 [16384, 768], P(('dp', 'tensor')), may hold values from -24 to 24, as said below
Outputs:
- layer_out: bfloat16 [16384, 768], P(('dp', 'tensor'))
- grad_tokens: bfloat16 [16384, 768], P(('dp', 'tensor'))
- grad_w_query: float32 [768, 768], P(None, 'tensor')
- grad_w_key: float32 [768, 768], P(None, 'tensor')
- grad_w_value: float32 [768, 768], P(None, 'tensor')
- grad_b_query: float32 [768], P('tensor')
- grad_b_value: float32 [768], P('tensor')
- grad_w_output: float32 [768, 768], P('tensor')
- grad_b_output: float32 [768], replicated
- grad_first_gain: float32 [768], replicated
- grad_first_shift: float32 [768], replicated
- grad_w_up: float32 [768, 3072], P(None, 'tensor')
- grad_b_up: float32 [3072], P('tensor')
- grad_w_down: float32 [3072, 768], P('tensor')
- grad_b_down: float32 [768], replicated
- grad_second_gain: float32 [768], replicated
- grad_second_shift: float32 [768], replicated
Inputs may be any that keep to these rules, and one draw needn't show every extreme that they name: cotangent of the layer's output.
All inputs are finite; a program needn't handle non-finite values.
Results may differ from a plain program's by a relative error of at most 0.013.
The roundings to bfloat16 on the way count: a program that leaves them out, or rounds other values in their place, can miss the bound.
Values may be sent and summed in bfloat16 or wider, within the bound.
No kernel may reach another device: no remote copies, remote signals or barrier semaphores. Data moves between devices by JAX's collectives and lax.ppermute only.
A program may use at most 128 MiB of HBM per device.

v0:
```python
import jax
import jax.numpy as jnp
from jax import lax
from jax.sharding import PartitionSpec as P

HEAD = 64
SEQ_LEN = 512


def layer_norm(values, gain_row, shift_row):
    center = values - jnp.mean(values, axis=-1, keepdims=True)
    spread = jnp.mean(center * center, axis=-1, keepdims=True)
    return center * lax.rsqrt(spread + 1e-12) * gain_row + shift_row


def gelu_exact(values):
    return jax.nn.gelu(values, approximate=False)


def contract_rows(left, right):
    return lax.dot_general(
        left, right, (((0,), (0,)), ((), ())), preferred_element_type=jnp.float32
    )


def contract_cols(left, right):
    return lax.dot_general(
        left, right, (((1,), (1,)), ((), ())), preferred_element_type=jnp.float32
    )


def attend_forward(packed):
    queries, key_rows, value_rows = packed
    scores = (
        jnp.einsum("qhd,khd->hqk", queries, key_rows, preferred_element_type=jnp.float32) * 0.125
    )
    highest = jnp.max(scores, axis=-1, keepdims=True)
    unnorm = jnp.exp(scores - highest)
    totals = jnp.sum(unnorm, axis=-1, keepdims=True)
    soft_probs = (unnorm / totals).astype(jnp.bfloat16)
    attended = jnp.einsum(
        "hqk,khd->qhd", soft_probs, value_rows, preferred_element_type=jnp.float32
    )
    return (attended.astype(jnp.bfloat16), highest + jnp.log(totals))


def attend_backward(packed):
    queries, key_rows, value_rows, grad_att, log_total = packed
    scores = (
        jnp.einsum("qhd,khd->hqk", queries, key_rows, preferred_element_type=jnp.float32) * 0.125
    )
    soft_probs = jnp.exp(scores - log_total)
    grad_prob = jnp.einsum("qhd,khd->hqk", grad_att, value_rows, preferred_element_type=jnp.float32)
    inner_sum = jnp.sum(soft_probs * grad_prob, axis=-1, keepdims=True)
    grad_score = (soft_probs * (grad_prob - inner_sum)).astype(jnp.bfloat16)
    grad_query = (
        jnp.einsum("hqk,khd->qhd", grad_score, key_rows, preferred_element_type=jnp.float32) * 0.125
    ).astype(jnp.bfloat16)
    grad_key = (
        jnp.einsum("hqk,qhd->khd", grad_score, queries, preferred_element_type=jnp.float32) * 0.125
    ).astype(jnp.bfloat16)
    grad_value = jnp.einsum(
        "hqk,qhd->khd",
        soft_probs.astype(jnp.bfloat16),
        grad_att,
        preferred_element_type=jnp.float32,
    ).astype(jnp.bfloat16)
    return (grad_query, grad_key, grad_value)


def on_device(
    tokens,
    w_query,
    w_key,
    w_value,
    b_query,
    b_value,
    w_output,
    b_output,
    first_gain,
    first_shift,
    w_up,
    b_up,
    w_down,
    b_down,
    second_gain,
    second_shift,
    cotangent,
):
    share_rows = tokens.shape[0]
    group_rows = share_rows * lax.axis_size("tensor")
    local_width = w_query.shape[1]
    local_heads = local_width // HEAD
    seq_count = group_rows // SEQ_LEN
    w_joined = jnp.concatenate([w_query, w_key, w_value], axis=1)
    b_joined = jnp.concatenate(
        [
            b_query.astype(jnp.float32),
            jnp.zeros((local_width,), jnp.float32),
            b_value.astype(jnp.float32),
        ]
    )

    def split_heads(block):
        return block.reshape(seq_count, SEQ_LEN, local_heads, HEAD)

    inputs_full = lax.all_gather(tokens, "tensor", axis=0, tiled=True)
    projected = (
        jnp.dot(inputs_full, w_joined, preferred_element_type=jnp.float32) + b_joined
    ).astype(jnp.bfloat16)
    queries = split_heads(projected[:, :local_width])
    key_rows = split_heads(projected[:, local_width : 2 * local_width])
    value_rows = split_heads(projected[:, 2 * local_width :])
    attended, log_total = lax.map(attend_forward, (queries, key_rows, value_rows))
    attended = attended.reshape(group_rows, local_width)
    picked = attended
    attention_part = lax.psum_scatter(
        jnp.dot(picked, w_output, preferred_element_type=jnp.float32),
        "tensor",
        scatter_dimension=0,
        tiled=True,
    )
    first_sum = attention_part + b_output.astype(jnp.float32) + tokens.astype(jnp.float32)
    normed, first_pull = jax.vjp(
        layer_norm, first_sum, first_gain.astype(jnp.float32), first_shift.astype(jnp.float32)
    )
    normed_low = normed.astype(jnp.bfloat16)
    normed_full = lax.all_gather(normed_low, "tensor", axis=0, tiled=True)
    up_rows = jnp.dot(normed_full, w_up, preferred_element_type=jnp.float32) + b_up.astype(
        jnp.float32
    )
    active, gelu_pull = jax.vjp(gelu_exact, up_rows)
    active = active.astype(jnp.bfloat16)
    picked = active
    feed_part = lax.psum_scatter(
        jnp.dot(picked, w_down, preferred_element_type=jnp.float32),
        "tensor",
        scatter_dimension=0,
        tiled=True,
    )
    second_sum = feed_part + b_down.astype(jnp.float32) + normed
    layer_out, second_pull = jax.vjp(
        layer_norm, second_sum, second_gain.astype(jnp.float32), second_shift.astype(jnp.float32)
    )
    grad_second, grad_second_gain, grad_second_shift = second_pull(cotangent.astype(jnp.float32))
    grad_b_down = jnp.sum(grad_second, axis=0)
    down_low = grad_second.astype(jnp.bfloat16)
    down_full = lax.all_gather(down_low, "tensor", axis=0, tiled=True)
    grad_w_down = contract_rows(active, down_full)
    grad_active = contract_cols(down_full, w_down)
    grad_up = gelu_pull(grad_active)[0].astype(jnp.bfloat16)
    grad_b_up = jnp.sum(grad_up, axis=0, dtype=jnp.float32)
    grad_w_up = contract_rows(normed_full, grad_up)
    picked = grad_up
    hidden_part = lax.psum_scatter(
        contract_cols(picked, w_up), "tensor", scatter_dimension=0, tiled=True
    )
    grad_normed = hidden_part + grad_second
    grad_first, grad_first_gain, grad_first_shift = first_pull(grad_normed)
    grad_b_output = jnp.sum(grad_first, axis=0)
    first_low = grad_first.astype(jnp.bfloat16)
    first_full = lax.all_gather(first_low, "tensor", axis=0, tiled=True)
    grad_w_output = contract_rows(attended, first_full)
    grad_att = contract_cols(first_full, w_output).astype(jnp.bfloat16)
    grad_query, grad_key, grad_value = lax.map(
        attend_backward, (queries, key_rows, value_rows, split_heads(grad_att), log_total)
    )
    grad_joined = jnp.concatenate(
        [
            grad_query.reshape(group_rows, local_width),
            grad_key.reshape(group_rows, local_width),
            grad_value.reshape(group_rows, local_width),
        ],
        axis=1,
    )
    grad_b_query = jnp.sum(grad_joined[:, :local_width], axis=0, dtype=jnp.float32)
    grad_b_value = jnp.sum(grad_joined[:, 2 * local_width :], axis=0, dtype=jnp.float32)
    grad_w_joined = contract_rows(inputs_full, grad_joined)
    picked = grad_joined
    input_part = lax.psum_scatter(
        contract_cols(picked, w_joined), "tensor", scatter_dimension=0, tiled=True
    )
    grad_tokens = (input_part + grad_first).astype(jnp.bfloat16)
    grad_w_query = grad_w_joined[:, :local_width]
    grad_w_key = grad_w_joined[:, local_width : 2 * local_width]
    grad_w_value = grad_w_joined[:, 2 * local_width :]
    (
        grad_w_query,
        grad_w_key,
        grad_w_value,
        grad_b_query,
        grad_b_value,
        grad_w_output,
        grad_w_up,
        grad_b_up,
        grad_w_down,
    ) = lax.psum(
        (
            grad_w_query,
            grad_w_key,
            grad_w_value,
            grad_b_query,
            grad_b_value,
            grad_w_output,
            grad_w_up,
            grad_b_up,
            grad_w_down,
        ),
        "dp",
    )
    (
        grad_b_output,
        grad_first_gain,
        grad_first_shift,
        grad_b_down,
        grad_second_gain,
        grad_second_shift,
    ) = lax.psum(
        (
            grad_b_output,
            grad_first_gain,
            grad_first_shift,
            grad_b_down,
            grad_second_gain,
            grad_second_shift,
        ),
        ("dp", "tensor"),
    )
    return (
        layer_out.astype(jnp.bfloat16),
        grad_tokens,
        grad_w_query,
        grad_w_key,
        grad_w_value,
        grad_b_query,
        grad_b_value,
        grad_w_output,
        grad_b_output,
        grad_first_gain,
        grad_first_shift,
        grad_w_up,
        grad_b_up,
        grad_w_down,
        grad_b_down,
        grad_second_gain,
        grad_second_shift,
    )


def solution(mesh):
    return jax.shard_map(
        on_device,
        mesh=mesh,
        in_specs=(
            P(("dp", "tensor"), None),
            P(None, "tensor"),
            P(None, "tensor"),
            P(None, "tensor"),
            P("tensor"),
            P("tensor"),
            P("tensor", None),
            P(),
            P(),
            P(),
            P(None, "tensor"),
            P("tensor"),
            P("tensor", None),
            P(),
            P(),
            P(),
            P(("dp", "tensor"), None),
        ),
        out_specs=(
            P(("dp", "tensor"), None),
            P(("dp", "tensor"), None),
            P(None, "tensor"),
            P(None, "tensor"),
            P(None, "tensor"),
            P("tensor"),
            P("tensor"),
            P("tensor", None),
            P(),
            P(),
            P(),
            P(None, "tensor"),
            P("tensor"),
            P("tensor", None),
            P(),
            P(),
            P(),
        ),
        check_vma=False,
    )
```

profile of v0, /device:TPU:0, one launch (start us, length us, event | category | flops | bytes accessed | tf_op | source)
XLA Modules:
  0.0 759.8 jit_solution(11368604049422810197)
XLA Ops:
  12.4 28.5 %all-gather.5.cloned.1.call-done = bf16[2048,768]{1,0:T(8,128)(2,1)} async-done(((bf16[512,768]{1,0:T(8,128)(2,1)}), bf16[2048,768]{1,0:T(8,128)(2,1)}) %all-gather.5.cloned.1.call-update) | async-done | bytes 3145744 | tf_op jit(solution)/shard_map/all_gather | solution.py:107
  40.9 3.9 fusion.63
  45.0 1.5 reshape.152
  47.7 1.5 reshape.153
  50.5 1.5 reshape.154
  54.2 12.9 %while.26 = (s32[]{:T(128)}, bf16[4,512,3,64]{1,3,2,0:T(8,128)(2,1)}, f32[4,3,512,1]{2,1,3,0:T(4,128)}, bf16[4,512,3,64]{1,3,2,0:T(8,128)(2,1)S(1)}, bf16[4,512,...) while((s32[]{:T(128)}, bf16[4,512,3,64]{1,3,2,0:T(8,128)(2,1)}, ...), condition=%wide.region_3.4_spmd, body=%wide.region_0.3_spmd.sunk | while | flops 208501248 | bytes 10281549 | solution.py:114
  56.0 1.4 fusion.128
  59.2 1.4 fusion.128
  62.4 1.4 fusion.128
  65.7 1.4 fusion.128
  67.1 2.3 copy.52
  70.5 3.7 fusion.78
  74.9 57.8 %reduce-scatter.5.cloned.1.call-done = f32[512,768]{1,0:T(8,128)} async-done(((f32[2048,768]{1,0:T(8,128)}), f32[512,768]{1,0:T(8,128)}) %reduce-scatter.5.cloned.1.call-update) | async-done | bytes 1572880 | tf_op jit(solution)/shard_map/reduce_scatter | solution.py:117
  132.8 1.9 fusion.75
  137.9 27.7 %all-gather.7.cloned.1.call-done = bf16[2048,768]{1,0:T(8,128)(2,1)} async-done(((bf16[512,768]{1,0:T(8,128)(2,1)}), bf16[2048,768]{1,0:T(8,128)(2,1)}) %all-gather.7.cloned.1.call-update) | async-done | bytes 3145744 | tf_op jit(solution)/shard_map/all_gather | solution.py:128
  165.5 18.4 %multiply_convert_fusion.1 = (bf16[2048,768]{1,0:T(8,128)(2,1)S(1)}, f32[2048,768]{1,0:T(8,128)}, f32[2048,768]{1,0:T(8,128)}) fusion(f32[768]{0:T(1024)S(1)} %convert_element_type.116, bf16[2048,768]{1,0:T(8,128)(2,1)} %all-gather.7.cloned.1.call-done, bf16[768,768]{1,0:T(8,128)(2,1)S(1)} %copy-done), kind=kOutput, calls=%fused_computation.64 | convolution fusion | flops 2519728128 | bytes 20057088 | tf_op jit(solution)/shard_map/dot_general | solution.py:129
  184.0 1.7 copy-done.40
  185.7 4.5 fusion.79
  193.4 55.3 %reduce-scatter.7.cloned.1.call-done = f32[512,768]{1,0:T(8,128)} async-done(((f32[2048,768]{1,0:T(8,128)}), f32[512,768]{1,0:T(8,128)}) %reduce-scatter.7.cloned.1.call-update) | async-done | bytes 1572880 | tf_op jit(solution)/shard_map/reduce_scatter | solution.py:135
  248.7 2.0 fusion.73
  252.3 1.6 fusion.72
  255.0 1.7 add_reduce_fusion.1
  257.3 28.1 %all-gather.9.cloned.1.call-done = bf16[2048,768]{1,0:T(8,128)(2,1)} async-done(((bf16[512,768]{1,0:T(8,128)(2,1)}), bf16[2048,768]{1,0:T(8,128)(2,1)}) %all-gather.9.cloned.1.call-update) | async-done | bytes 3145744 | tf_op jit(solution)/shard_map/all_gather | solution.py:148
  285.4 11.0 %convert_reduce_fusion = (f32[768]{0:T(1024)}, bf16[2048,768]{1,0:T(8,128)(2,1)S(1)}) fusion(f32[2048,768]{1,0:T(8,128)} %get-tuple-element.195, f32[2048,768]{1,0:T(8,128)} %get-tuple-element.213, f32[768]{0:T(1024)} %copy-done.32, bf16[2048,768]{1,0:T(8,128)(2,1)} %all-gather.9.cloned.1.call-done, bf16[768,768]{1,0:T(8,128)(2,1)} %param.33), kind=kOutput, calls=%fused_computation.62 | convolution fusion | flops 2442657024 | bytes 20060160 | tf_op jit(solution)/shard_map/dot_general | solution.py:27
  296.5 1.7 copy-done.41
  298.1 4.5 fusion.80
  302.7 58.5 %reduce-scatter.9.cloned.1.call-done = f32[512,768]{1,0:T(8,128)} async-done(((f32[2048,768]{1,0:T(8,128)}), f32[512,768]{1,0:T(8,128)}) %reduce-scatter.9.cloned.1.call-update) | async-done | bytes 1572880 | tf_op jit(solution)/shard_map/reduce_scatter | solution.py:155
  361.2 3.3 multiply_reduce_fusion.2
  367.7 28.5 %all-gather.11.cloned.1.call-done = bf16[2048,768]{1,0:T(8,128)(2,1)} async-done(((bf16[512,768]{1,0:T(8,128)(2,1)}), bf16[2048,768]{1,0:T(8,128)(2,1)}) %all-gather.11.cloned.1.call-update) | async-done | bytes 3145744 | tf_op jit(solution)/shard_map/all_gather | solution.py:162
  396.2 3.1 convolution_convert_fusion
  402.0 27.8 %while.27 = (s32[]{:T(128)}, bf16[4,512,3,64]{1,3,2,0:T(8,128)(2,1)S(1)}, bf16[4,512,3,64]{1,3,2,0:T(8,128)(2,1)}, bf16[4,512,3,64]{1,3,2,0:T(8,128)(2,1)}, bf16...) while((s32[]{:T(128)}, ...), condition=%wide.region_17.18_spmd, body=%wide.region_15.17_spmd.sunk | while | flops 513243648 | bytes 25611368 | solution.py:165
  403.3 1.7 multiply_reduce_fusion.9
  410.3 1.7 multiply_reduce_fusion.9
  417.2 1.7 multiply_reduce_fusion.9
  424.2 1.7 multiply_reduce_fusion.9
  431.7 1.8 copy.59
  435.3 4.6 fusion.81
  440.2 7.0 fusion.84
  447.2 4.2 fusion.83
  451.4 2.0 convolution_bitcast_fusion
  455.1 1.6 fusion.82
  457.4 40.8 %all-reduce = (f32[768]{0:T(1024)}, f32[768]{0:T(1024)}, f32[768]{0:T(1024)}, f32[768]{0:T(1024)}, f32[768]{0:T(1024)}, /*index=5*/f32[768]{0:T(1024)}) all-reduce(f32[768]{0:T(1024)S(1)} %get-tuple-element.211, f32[768]{0:T(1024)S(1)} %copy-done.29, f32[768]{0:T(1024)S(1)} %copy-done.30, ...), channel_id=1, replica_groups=mesh['dp'=8,'tensor'=4] {'dp','tensor'}, use_global_device_ids=true, to_apply=%region_28.29 | all-reduce | flops 4608 | bytes 36864 | tf_op jit(solution)/shard_map/psum | solution.py:218
  499.9 22.2 %all-reduce.1 = (f32[192]{0:T(256)}, f32[192]{0:T(256)}, f32[768]{0:T(1024)}) all-reduce(f32[192]{0:T(256)S(1)} %reduce_sum.216, f32[192]{0:T(256)S(1)} %reduce_sum.218, f32[768]{0:T(1024)S(1)} %copy-done.31), channel_id=1, replica_groups=mesh['dp'=8,'tensor'=4] {'dp'}, use_global_device_ids=true, to_apply=%region_23.24 | all-reduce | flops 1152 | bytes 9216 | tf_op jit(solution)/shard_map/psum | solution.py:197
  522.1 2.5 add_convert_fusion.2
  524.6 218.8 %all-reduce.5.cloned.1.call-done = (f32[768,192]{0,1:T(8,128)}, f32[768,192]{0,1:T(8,128)}, f32[768,192]{0,1:T(8,128)}, f32[192,768]{1,0:T(8,128)}, f32[768,768]{1,0:T(8,128)}, /*index=5*/f32[768,768]{1,0:T(8,128)}) async-done(((f32[768,192]{0,1:T(8,128)}, f32[768,192]{0,1:T(8,128)}, f32[768,192]{0,1:T(8,128)}, f32[192,768]{1,0:T(8,128)}, f32[768,768]{1,0:T(8,128)}, /*index=5*/f32[768,768]{1,0:T(8,128)}), ...) | async-done | bytes 7077904 | tf_op jit(solution)/shard_map/psum | solution.py:197
  743.5 2.1 copy.106
  745.5 1.9 copy.107
  747.4 1.9 copy.108
  (194 shorter events, 66.8 us)
Async XLA Ops:
  7.2 158.3 %copy-start = (bf16[768,768]{1,0:T(8,128)(2,1)S(1)}, bf16[768,768]{1,0:T(8,128)(2,1)}, u32[]{:S(2)}) copy-start(bf16[768,768]{1,0:T(8,128)(2,1)} %param.31) | copy-start | bytes 3538948
  7.2 33.7 %all-gather.5.cloned.1.call-start = ((), (), s32[]{:S(2)}) async-start(), calls=%async_computation.4 | async-start | bytes 3932160 | tf_op jit(solution)/shard_map/all_gather | solution.py:107
  7.9 124.8 %reduce-scatter.5.cloned.1.call-start = ((), (), s32[]{:S(2)}) async-start(), calls=%async_computation.5 | async-start | bytes 7864320 | tf_op jit(solution)/shard_map/reduce_scatter | solution.py:117
  12.4 28.5 %copy-start.20 = (bf16[768,576]{0,1:T(8,128)(2,1)}, bf16[768,576]{0,1:T(8,128)(2,1)S(1)}, u32[]{:S(2)}) copy-start(bf16[768,576]{0,1:T(8,128)(2,1)S(1)} %constant_dynamic-update-slice_fusion) | copy-start | bytes 2654212
  67.1 7.1 copy-start.2
  67.1 7.1 copy-start.9
  67.1 3.4 copy-start.16
  69.6 0.9 copy-start.7
  74.2 0.7 copy-start.34
  74.2 0.7 copy-start.35
  74.3 91.3 %all-gather.7.cloned.1.call-start = ((), (), s32[]{:S(2)}) async-start(), calls=%async_computation.6 | async-start | bytes 3932160 | tf_op jit(solution)/shard_map/all_gather | solution.py:128
  74.9 61.9 %copy-start.22 = (f32[768]{0:T(1024)}, f32[768]{0:T(1024)S(1)}, u32[]{:S(2)}) copy-start(f32[768]{0:T(1024)S(1)} %convert_element_type.114) | copy-start | bytes 9220
  136.8 111.9 %reduce-scatter.7.cloned.1.call-start = ((), (), s32[]{:S(2)}) async-start(), calls=%async_computation.7 | async-start | bytes 7864320 | tf_op jit(solution)/shard_map/reduce_scatter | solution.py:135
  137.9 46.1 %copy-start.32 = (f32[768]{0:T(1024)}, f32[768]{0:T(1024)S(1)}, u32[]{:S(2)}) copy-start(f32[768]{0:T(1024)S(1)} %convert_element_type.116) | copy-start | bytes 9220
  165.5 20.2 %copy-start.39 = (bf16[768,768]{1,0:T(8,128)(2,1)S(1)}, bf16[768,768]{1,0:T(8,128)(2,1)}, u32[]{:S(2)}) copy-start(bf16[768,768]{1,0:T(8,128)(2,1)} %param.33) | copy-start | bytes 3538948
  184.0 1.7 copy-start.40
  190.2 95.3 %all-gather.9.cloned.1.call-start = ((), (), s32[]{:S(2)}) async-start(), calls=%async_computation.8 | async-start | bytes 3932160 | tf_op jit(solution)/shard_map/all_gather | solution.py:148
  248.7 2.4 copy-start.11
  250.7 1.6 copy-start.25
  253.9 1.1 copy-start.6
  256.7 104.5 %reduce-scatter.9.cloned.1.call-start = ((), (), s32[]{:S(2)}) async-start(), calls=%async_computation.9 | async-start | bytes 7864320 | tf_op jit(solution)/shard_map/reduce_scatter | solution.py:155
  296.5 1.7 copy-start.41
  302.7 61.8 %copy-start.24 = (f32[512]{0:T(512)S(1)}, f32[512]{0:T(512)}, u32[]{:S(2)}) copy-start(f32[512]{0:T(512)} %copy-done.23) | copy-start | bytes 6148
  302.7 93.5 %all-gather.11.cloned.1.call-start = ((), (), s32[]{:S(2)}) async-start(), calls=%async_computation.10 | async-start | bytes 3932160 | tf_op jit(solution)/shard_map/all_gather | solution.py:162
  364.5 31.7 %copy-start.17 = (bf16[192,768]{1,0:T(8,128)(2,1)S(1)}, bf16[192,768]{1,0:T(8,128)(2,1)}, u32[]{:S(2)}) copy-start(bf16[192,768]{1,0:T(8,128)(2,1)} %param.27) | copy-start | bytes 884740
  365.2 1.2 copy-start.4
  367.5 154.6 %reduce-scatter.11.cloned.1.call-start = ((), (), s32[]{:S(2)}) async-start(), calls=%async_computation.11 | async-start | bytes 7864320 | tf_op jit(solution)/shard_map/reduce_scatter | solution.py:180
  399.2 2.7 copy-start.3
  429.8 1.1 copy-start.12
  431.7 3.6 copy-start.21
  433.9 1.4 copy-start.18
  439.9 303.6 %all-reduce.5.cloned.1.call-start = ((), (), s32[]{:S(2)}) async-start(), calls=%async_computation.12 | async-start | bytes 14155776 | tf_op jit(solution)/shard_map/psum | solution.py:197
  440.1 7.1 copy-start.38
  440.2 7.1 copy-start.42
  447.2 4.2 copy-start.19
  447.2 4.2 copy-start.37
  451.4 3.3 copy-start.10
  453.4 1.6 copy-start.8
  456.7 0.7 copy-start.27
  456.7 0.7 copy-start.28
  456.7 0.7 copy-start.29
  456.7 0.7 copy-start.30
  456.7 43.1 %copy-start.31 = (f32[768]{0:T(1024)S(1)}, f32[768]{0:T(1024)}, u32[]{:S(2)}) copy-start(f32[768]{0:T(1024)} %get-tuple-element.185) | copy-start | bytes 9220
  456.7 65.4 %copy-start.5 = (f32[512,768]{1,0:T(8,128)S(1)}, f32[512,768]{1,0:T(8,128)}, u32[]{:S(2)}) copy-start(f32[512,768]{1,0:T(8,128)} %copy-done.4) | copy-start | bytes 4718596
  743.5 5.9 copy-start.15
  743.5 6.7 copy-start.14
  749.4 2.2 copy-start.13
  750.2 2.8 copy-start.1
  (4 other events, 2.6 us)
Sparse Core Ops, SparseCore 0:
  9.6 31.2 all-gather.4
  74.4 58.3 reduce-scatter.4
  137.0 28.5 all-gather.6
  190.3 58.3 reduce-scatter.6
  256.9 28.5 all-gather.8
  302.8 58.3 reduce-scatter.8
  367.6 28.5 all-gather.10
  440.0 59.7 reduce-scatter.10
  506.0 237.3 all-reduce.4
where the time goes:
time: 768 us; the launch traced here: 760 us
  waiting for transfers between devices  504 us (66%)
  matrix products  98.3 us (13%)
  blocking collectives  63.1 us (8%)
  local copies, waits for them, and re-layouts  46.3 us (6%)
  other arithmetic  31.9 us (4%)
  between operations  14.5 us (2%)
    psum x1, waiting for transfers between devices, on_device(): lax.psum((grad_w_query, grad_w_key, grad_w_value, grad_b_query, grad_b_va...  219 us
    reduce_scatter x1, waiting for transfers between devices, on_device(): lax.psum_scatter(contract_cols(picked, w_up), 'tensor', scatter_dimension...  58.5 us
    reduce_scatter x1, waiting for transfers between devices, on_device(): lax.psum_scatter(jnp.dot(picked, w_output, preferred_element_type=jnp.flo...  57.8 us
    reduce_scatter x1, waiting for transfers between devices, on_device(): lax.psum_scatter(jnp.dot(picked, w_down, preferred_element_type=jnp.float...  55.3 us
    psum x1, blocking collectives, on_device(): lax.psum((grad_b_output, grad_first_gain, grad_first_shift, grad_b_down,...  40.8 us
    all_gather x1, waiting for transfers between devices, on_device(): inputs_full = lax.all_gather(tokens, 'tensor', axis=0, tiled=True)  28.5 us
    all_gather x1, waiting for transfers between devices, on_device(): first_full = lax.all_gather(first_low, 'tensor', axis=0, tiled=True)  28.5 us
    all_gather x1, waiting for transfers between devices, on_device(): down_full = lax.all_gather(down_low, 'tensor', axis=0, tiled=True)  28.1 us
  transfers between devices with their start and end apart: 9, of which 8 were waited for; matrix products, arithmetic and copies ran while one was open for 4% of the time, Pallas kernels for 0%

commit v1 on v0

--- a/solution.py
+++ b/solution.py
@@ -159,7 +159,14 @@
     grad_first, grad_first_gain, grad_first_shift = first_pull(grad_normed)
     grad_b_output = jnp.sum(grad_first, axis=0)
     first_low = grad_first.astype(jnp.bfloat16)
-    first_full = lax.all_gather(first_low, "tensor", axis=0, tiled=True)
+    size = lax.axis_size("tensor")
+    route = [(i, (i + 1) % size) for i in range(size)]
+    terms = [first_low]
+    for reach in range(1, size):
+        terms = [lax.ppermute(terms[0], "tensor", route), *terms]
+    out = jnp.concatenate(terms, axis=0)
+    shift = (lax.axis_index("tensor") + 1) * terms[-1].shape[0]
+    first_full = jnp.roll(out, shift, axis=0)
     grad_w_output = contract_rows(attended, first_full)
     grad_att = contract_cols(first_full, w_output).astype(jnp.bfloat16)
     grad_query, grad_key, grad_value = lax.map(

time: 768 us -> 776 us (1.010)
    ppermute x0 -> x3, waiting for transfers between devices: none -> 34.3 us  [on_device(): terms = [lax.ppermute(terms[0], 'tensor', route), *terms]]
    all_gather x1 -> x0, waiting for transfers between devices: 28.5 us -> none  [on_device(): first_full = lax.all_gather(first_low, 'tensor', axis=0, tiled=True)]
    unnamed x100 -> x111, local copies, waits for them, and re-layouts: 23.6 us -> 27.8 us
  transfers between devices with their start and end apart: 9 -> 11, of which waited for: 8 -> 10; matrix products, arithmetic and copies ran while one was open for 4% -> 4% of each run, Pallas kernels for 0% -> 0%
where the time goes in v1:
time: 776 us; the launch traced here: 768 us
  waiting for transfers between devices  511 us (66%)
  matrix products  96.6 us (12%)
  blocking collectives  62.9 us (8%)
  local copies, waits for them, and re-layouts  50.5 us (7%)
  other arithmetic  30.5 us (4%)
  between operations  14.9 us (2%)
    psum x1, waiting for transfers between devices, on_device(): lax.psum((grad_w_query, grad_w_key, grad_w_value, grad_b_query, grad_b_va...  220 us
    reduce_scatter x1, waiting for transfers between devices, on_device(): lax.psum_scatter(contract_cols(picked, w_up), 'tensor', scatter_dimension...  58.5 us
    reduce_scatter x1, waiting for transfers between devices, on_device(): lax.psum_scatter(jnp.dot(picked, w_output, preferred_element_type=jnp.flo...  57.8 us
    reduce_scatter x1, waiting for transfers between devices, on_device(): lax.psum_scatter(jnp.dot(picked, w_down, preferred_element_type=jnp.float...  55.2 us
    psum x1, blocking collectives, on_device(): lax.psum((grad_b_output, grad_first_gain, grad_first_shift, grad_b_down,...  40.5 us
    ppermute x3, waiting for transfers between devices, on_device(): terms = [lax.ppermute(terms[0], 'tensor', route), *terms]  34.3 us
    all_gather x1, waiting for transfers between devices, on_device(): inputs_full = lax.all_gather(tokens, 'tensor', axis=0, tiled=True)  28.5 us
    all_gather x1, waiting for transfers between devices, on_device(): down_full = lax.all_gather(down_low, 'tensor', axis=0, tiled=True)  28.1 us
  transfers between devices with their start and end apart: 11, of which 10 were waited for; matrix products, arithmetic and copies ran while one was open for 4% of the time, Pallas kernels for 0%

profile of v1, /device:TPU:0, one launch (start us, length us, event | category | flops | bytes accessed | tf_op | source)
XLA Modules:
  0.0 768.1 jit_solution(12621473764738463100)
XLA Ops:
  12.4 28.5 %all-gather.4.cloned.1.call-done = bf16[2048,768]{1,0:T(8,128)(2,1)} async-done(((bf16[512,768]{1,0:T(8,128)(2,1)}), bf16[2048,768]{1,0:T(8,128)(2,1)}) %all-gather.4.cloned.1.call-update) | async-done | bytes 3145744 | tf_op jit(solution)/shard_map/all_gather | solution.py:107
  40.9 3.9 fusion.63
  45.0 1.5 reshape.154
  50.5 1.5 reshape.152
  54.2 12.9 %while.26 = (s32[]{:T(128)}, bf16[4,512,3,64]{1,3,2,0:T(8,128)(2,1)}, f32[4,3,512,1]{2,1,3,0:T(4,128)}, bf16[4,512,3,64]{1,3,2,0:T(8,128)(2,1)S(1)}, bf16[4,512,...) while((s32[]{:T(128)}, bf16[4,512,3,64]{1,3,2,0:T(8,128)(2,1)}, ...), condition=%wide.region_3.4_spmd, body=%wide.region_0.3_spmd.sunk | while | flops 208501248 | bytes 10281049 | solution.py:114
  55.3 1.5 fusion.134
  58.6 1.5 fusion.134
  65.0 1.5 fusion.134
  67.1 2.3 copy.52
  70.5 3.7 fusion.87
  75.0 57.8 %reduce-scatter.5.cloned.1.call-done = f32[512,768]{1,0:T(8,128)} async-done(((f32[2048,768]{1,0:T(8,128)}), f32[512,768]{1,0:T(8,128)}) %reduce-scatter.5.cloned.1.call-update) | async-done | bytes 1572880 | tf_op jit(solution)/shard_map/reduce_scatter | solution.py:117
  132.8 1.9 fusion.84
  137.9 27.7 %all-gather.6.cloned.1.call-done = bf16[2048,768]{1,0:T(8,128)(2,1)} async-done(((bf16[512,768]{1,0:T(8,128)(2,1)}), bf16[2048,768]{1,0:T(8,128)(2,1)}) %all-gather.6.cloned.1.call-update) | async-done | bytes 3145744 | tf_op jit(solution)/shard_map/all_gather | solution.py:128
  165.5 18.5 %multiply_convert_fusion.1 = (bf16[2048,768]{1,0:T(8,128)(2,1)S(1)}, f32[2048,768]{1,0:T(8,128)}, f32[2048,768]{1,0:T(8,128)}) fusion(f32[768]{0:T(1024)S(1)} %convert_element_type.116, bf16[2048,768]{1,0:T(8,128)(2,1)} %all-gather.6.cloned.1.call-done, bf16[768,768]{1,0:T(8,128)(2,1)S(1)} %copy-done), kind=kOutput, calls=%fused_computation.64 | convolution fusion | flops 2519728128 | bytes 20057088 | tf_op jit(solution)/shard_map/dot_general | solution.py:129
  184.0 1.7 copy-done.40
  185.7 4.5 fusion.88
  193.5 55.2 %reduce-scatter.7.cloned.1.call-done = f32[512,768]{1,0:T(8,128)} async-done(((f32[2048,768]{1,0:T(8,128)}), f32[512,768]{1,0:T(8,128)}) %reduce-scatter.7.cloned.1.call-update) | async-done | bytes 1572880 | tf_op jit(solution)/shard_map/reduce_scatter | solution.py:135
  248.7 2.0 fusion.82
  252.3 1.6 fusion.81
  255.1 1.7 add_reduce_fusion.1
  257.4 28.1 %all-gather.8.cloned.1.call-done = bf16[2048,768]{1,0:T(8,128)(2,1)} async-done(((bf16[512,768]{1,0:T(8,128)(2,1)}), bf16[2048,768]{1,0:T(8,128)(2,1)}) %all-gather.8.cloned.1.call-update) | async-done | bytes 3145744 | tf_op jit(solution)/shard_map/all_gather | solution.py:148
  285.5 11.0 %convert_reduce_fusion = (f32[768]{0:T(1024)}, bf16[2048,768]{1,0:T(8,128)(2,1)S(1)}) fusion(f32[2048,768]{1,0:T(8,128)} %get-tuple-element.195, f32[2048,768]{1,0:T(8,128)} %get-tuple-element.213, f32[768]{0:T(1024)} %copy-done.33, bf16[2048,768]{1,0:T(8,128)(2,1)} %all-gather.8.cloned.1.call-done, bf16[768,768]{1,0:T(8,128)(2,1)} %param.33), kind=kOutput, calls=%fused_computation.62 | convolution fusion | flops 2442657024 | bytes 20060160 | tf_op jit(solution)/shard_map/dot_general | solution.py:27
  296.5 1.6 copy-done.41
  298.1 4.5 fusion.89
  302.7 58.5 %reduce-scatter.9.cloned.1.call-done = f32[512,768]{1,0:T(8,128)} async-done(((f32[2048,768]{1,0:T(8,128)}), f32[512,768]{1,0:T(8,128)}) %reduce-scatter.9.cloned.1.call-update) | async-done | bytes 1572880 | tf_op jit(solution)/shard_map/reduce_scatter | solution.py:155
  361.2 3.3 multiply_reduce_fusion.2
  366.6 11.4 %collective-permute-done = bf16[512,768]{1,0:T(8,128)(2,1)S(1)} collective-permute-done((bf16[512,768]{1,0:T(8,128)(2,1)S(1)}, bf16[512,768]{1,0:T(8,128)(2,1)S(1)}, u32[]{:S(2)}, u32[]{:S(2)}) %collective-permute-start) | collective-permute-done | bytes 786464 | tf_op jit(solution)/shard_map/ppermute | solution.py:166
  378.0 11.4 %collective-permute-done.1 = bf16[512,768]{1,0:T(8,128)(2,1)S(1)} collective-permute-done((bf16[512,768]{1,0:T(8,128)(2,1)S(1)}, bf16[512,768]{1,0:T(8,128)(2,1)S(1)}, u32[]{:S(2)}, u32[]{:S(2)}) %collective-permute-start.1) | collective-permute-done | bytes 786464 | tf_op jit(solution)/shard_map/ppermute | solution.py:166
  389.6 11.5 %collective-permute-done.2 = bf16[512,768]{1,0:T(8,128)(2,1)} collective-permute-done((bf16[512,768]{1,0:T(8,128)(2,1)S(1)}, bf16[512,768]{1,0:T(8,128)(2,1)}, u32[]{:S(2)}, u32[]{:S(2)}) %collective-permute-start.2) | collective-permute-done | bytes 786464 | tf_op jit(solution)/shard_map/ppermute | solution.py:166
  403.9 2.6 copy-done.13
  410.4 27.8 %while.27 = (s32[]{:T(128)}, bf16[4,512,3,64]{1,3,2,0:T(8,128)(2,1)}, bf16[4,512,3,64]{1,3,2,0:T(8,128)(2,1)}, bf16[4,512,3,64]{1,3,2,0:T(8,128)(2,1)S(1)}, bf16...) while((s32[]{:T(128)}, ...), condition=%wide.region_17.18_spmd, body=%wide.region_15.17_spmd.sunk | while | flops 513243648 | bytes 25611376 | solution.py:172
  412.4 1.7 multiply_reduce_fusion.9
  419.3 1.7 multiply_reduce_fusion.9
  426.3 1.7 multiply_reduce_fusion.9
  433.2 1.7 multiply_reduce_fusion.9
  438.2 1.8 copy.58
  443.4 4.6 fusion.90
  448.3 7.2 fusion.92
  455.5 4.2 fusion.91
  459.7 1.7 fusion.64
  461.6 2.0 convolution_bitcast_fusion
  465.6 40.5 %all-reduce = (f32[768]{0:T(1024)}, f32[768]{0:T(1024)}, f32[768]{0:T(1024)}, f32[768]{0:T(1024)}, f32[768]{0:T(1024)}, /*index=5*/f32[768]{0:T(1024)}) all-reduce(f32[768]{0:T(1024)S(1)} %get-tuple-element.211, f32[768]{0:T(1024)S(1)} %copy-done.30, f32[768]{0:T(1024)S(1)} %copy-done.31, ...), channel_id=1, replica_groups=mesh['dp'=8,'tensor'=4] {'dp','tensor'}, use_global_device_ids=true, to_apply=%region_28.29 | all-reduce | flops 4608 | bytes 36864 | tf_op jit(solution)/shard_map/psum | solution.py:225
  506.6 22.4 %all-reduce.1 = (f32[192]{0:T(256)}, f32[192]{0:T(256)}, f32[768]{0:T(1024)}) all-reduce(f32[192]{0:T(256)S(1)} %reduce_sum.216, f32[192]{0:T(256)S(1)} %reduce_sum.218, f32[768]{0:T(1024)S(1)} %copy-done.32), channel_id=1, replica_groups=mesh['dp'=8,'tensor'=4] {'dp'}, use_global_device_ids=true, to_apply=%region_23.24 | all-reduce | flops 1152 | bytes 9216 | tf_op jit(solution)/shard_map/psum | solution.py:204
  529.0 2.5 add_convert_fusion.2
  531.5 220.0 %all-reduce.5.cloned.1.call-done = (f32[768,192]{0,1:T(8,128)}, f32[768,192]{0,1:T(8,128)}, f32[768,192]{0,1:T(8,128)}, f32[192,768]{1,0:T(8,128)}, f32[768,768]{1,0:T(8,128)}, /*index=5*/f32[768,768]{1,0:T(8,128)}) async-done(((f32[768,192]{0,1:T(8,128)}, f32[768,192]{0,1:T(8,128)}, f32[768,192]{0,1:T(8,128)}, f32[192,768]{1,0:T(8,128)}, f32[768,768]{1,0:T(8,128)}, /*index=5*/f32[768,768]{1,0:T(8,128)}), ...) | async-done | bytes 7077904 | tf_op jit(solution)/shard_map/psum | solution.py:204
  751.5 2.1 copy.113
  753.5 1.9 copy.114
  755.4 1.9 copy.115
  (210 shorter events, 71.1 us)
Async XLA Ops:
  7.2 158.4 %copy-start = (bf16[768,768]{1,0:T(8,128)(2,1)S(1)}, bf16[768,768]{1,0:T(8,128)(2,1)}, u32[]{:S(2)}) copy-start(bf16[768,768]{1,0:T(8,128)(2,1)} %param.31) | copy-start | bytes 3538948
  7.2 33.7 %all-gather.4.cloned.1.call-start = ((), (), s32[]{:S(2)}) async-start(), calls=%async_computation.4 | async-start | bytes 3932160 | tf_op jit(solution)/shard_map/all_gather | solution.py:107
  7.9 124.9 %reduce-scatter.5.cloned.1.call-start = ((), (), s32[]{:S(2)}) async-start(), calls=%async_computation.5 | async-start | bytes 7864320 | tf_op jit(solution)/shard_map/reduce_scatter | solution.py:117
  12.4 28.5 %copy-start.21 = (bf16[768,576]{0,1:T(8,128)(2,1)}, bf16[768,576]{0,1:T(8,128)(2,1)S(1)}, u32[]{:S(2)}) copy-start(bf16[768,576]{0,1:T(8,128)(2,1)S(1)} %constant_dynamic-update-slice_fusion) | copy-start | bytes 2654212
  67.1 7.1 copy-start.2
  67.1 7.1 copy-start.11
  67.1 3.4 copy-start.17
  69.6 0.9 copy-start.7
  74.3 91.3 %all-gather.6.cloned.1.call-start = ((), (), s32[]{:S(2)}) async-start(), calls=%async_computation.6 | async-start | bytes 3932160 | tf_op jit(solution)/shard_map/all_gather | solution.py:128
  74.9 61.9 %copy-start.23 = (f32[768]{0:T(1024)}, f32[768]{0:T(1024)S(1)}, u32[]{:S(2)}) copy-start(f32[768]{0:T(1024)S(1)} %convert_element_type.114) | copy-start | bytes 9220
  136.9 111.9 %reduce-scatter.7.cloned.1.call-start = ((), (), s32[]{:S(2)}) async-start(), calls=%async_computation.7 | async-start | bytes 7864320 | tf_op jit(solution)/shard_map/reduce_scatter | solution.py:135
  137.9 46.1 %copy-start.33 = (f32[768]{0:T(1024)}, f32[768]{0:T(1024)S(1)}, u32[]{:S(2)}) copy-start(f32[768]{0:T(1024)S(1)} %convert_element_type.116) | copy-start | bytes 9220
  165.5 20.2 %copy-start.39 = (bf16[768,768]{1,0:T(8,128)(2,1)S(1)}, bf16[768,768]{1,0:T(8,128)(2,1)}, u32[]{:S(2)}) copy-start(bf16[768,768]{1,0:T(8,128)(2,1)} %param.33) | copy-start | bytes 3538948
  184.0 1.7 copy-start.40
  190.2 95.3 %all-gather.8.cloned.1.call-start = ((), (), s32[]{:S(2)}) async-start(), calls=%async_computation.8 | async-start | bytes 3932160 | tf_op jit(solution)/shard_map/all_gather | solution.py:148
  248.7 2.4 copy-start.12
  250.8 1.6 copy-start.26
  253.9 1.1 copy-start.6
  256.8 104.4 %reduce-scatter.9.cloned.1.call-start = ((), (), s32[]{:S(2)}) async-start(), calls=%async_computation.9 | async-start | bytes 7864320 | tf_op jit(solution)/shard_map/reduce_scatter | solution.py:155
  296.5 1.6 copy-start.41
  302.7 61.8 %copy-start.25 = (f32[512]{0:T(512)S(1)}, f32[512]{0:T(512)}, u32[]{:S(2)}) copy-start(f32[512]{0:T(512)} %copy-done.24) | copy-start | bytes 6148
  302.7 226.3 %reduce-scatter.11.cloned.1.call-start = ((), (), s32[]{:S(2)}) async-start(), calls=%async_computation.10 | async-start | bytes 7864320 | tf_op jit(solution)/shard_map/reduce_scatter | solution.py:187
  365.1 1.1 copy-start.4
  366.5 11.5 %collective-permute-start = (bf16[512,768]{1,0:T(8,128)(2,1)S(1)}, bf16[512,768]{1,0:T(8,128)(2,1)S(1)}, u32[]{:S(2)}, u32[]{:S(2)}) collective-permute-start(bf16[512,768]{1,0:T(8,128)(2,1)S(1)} %get-tuple-element.212), channel_id=1, source_target_pairs={{0,1},{1,2},{2,3},{3,0},{4,5},{5,6},{6,7},{7,4},{8,9},{9,10},{10,1... | collective-permute-start | bytes 2359304 | tf_op jit(solution)/shard_map/ppermute | solution.py:166
  378.0 11.4 %collective-permute-start.1 = (bf16[512,768]{1,0:T(8,128)(2,1)S(1)}, bf16[512,768]{1,0:T(8,128)(2,1)S(1)}, u32[]{:S(2)}, u32[]{:S(2)}) collective-permute-start(bf16[512,768]{1,0:T(8,128)(2,1)S(1)} %collective-permute-done), channel_id=1, source_target_pairs={{0,1},{1,2},{2,3},{3,0},{4,5},{5,6},{6,7},{7,4},{8,9},{9,10},{10,1... | collective-permute-start | bytes 2359304 | tf_op jit(solution)/shard_map/ppermute | solution.py:166
  389.4 11.7 %collective-permute-start.2 = (bf16[512,768]{1,0:T(8,128)(2,1)S(1)}, bf16[512,768]{1,0:T(8,128)(2,1)}, u32[]{:S(2)}, u32[]{:S(2)}) collective-permute-start(bf16[512,768]{1,0:T(8,128)(2,1)S(1)} %collective-permute-done.1), channel_id=1, source_target_pairs={{0,1},{1,2},{2,3},{3,0},{4,5},{5,6},{6,7},{7,4},{8,9},{9,10},{10,1... | collective-permute-start | bytes 2359304 | tf_op jit(solution)/shard_map/ppermute | solution.py:166
  402.4 4.1 copy-start.18
  403.8 2.6 copy-start.13
  407.7 2.7 copy-start.3
  438.2 2.0 copy-start.9
  441.6 1.8 copy-start.22
  442.0 1.4 copy-start.19
  448.0 303.5 %all-reduce.5.cloned.1.call-start = ((), (), s32[]{:S(2)}) async-start(), calls=%async_computation.11 | async-start | bytes 14155776 | tf_op jit(solution)/shard_map/psum | solution.py:204
  448.2 7.2 copy-start.38
  448.2 7.2 copy-start.42
  448.3 11.4 %slice-start = ((s8[6291456]{0:T(1024)(128)(4,1)}), s8[4194304]{0:T(1024)(128)(4,1)S(1)}, s32[]{:S(2)}) async-start(s8[6291456]{0:T(1024)(128)(4,1)} %bitcast.164), calls=%async_computation.12 | async-start | bytes 8388608
  455.4 4.2 copy-start.8
  455.4 4.2 slice-start.1
  455.5 5.9 copy-start.37
  459.6 1.9 copy-start.20
  464.9 0.7 copy-start.31
  464.9 41.3 %copy-start.10 = (bf16[4,512,3,64]{1,3,2,0:T(8,128)(2,1)S(1)}, bf16[4,512,3,64]{1,3,2,0:T(8,128)(2,1)}, u32[]{:S(2)}) copy-start(bf16[4,512,3,64]{1,3,2,0:T(8,128)(2,1)} %get-tuple-element.101) | copy-start | bytes 2359300
  464.9 41.7 %copy-start.32 = (f32[768]{0:T(1024)S(1)}, f32[768]{0:T(1024)}, u32[]{:S(2)}) copy-start(f32[768]{0:T(1024)} %get-tuple-element.185) | copy-start | bytes 9220
  464.9 64.1 %copy-start.5 = (f32[512,768]{1,0:T(8,128)S(1)}, f32[512,768]{1,0:T(8,128)}, u32[]{:S(2)}) copy-start(f32[512,768]{1,0:T(8,128)} %copy-done.4) | copy-start | bytes 4718596
  751.4 5.9 copy-start.16
  751.4 6.7 copy-start.15
  757.4 2.2 copy-start.14
  758.2 2.8 copy-start.1
  (8 other events, 5.5 us)
Sparse Core Ops, SparseCore 0:
  9.6 31.2 all-gather.3
  74.4 58.3 reduce-scatter.4
  137.0 28.5 all-gather.5
  190.3 58.3 reduce-scatter.6
  256.9 28.5 all-gather.7
  302.8 58.3 reduce-scatter.8
  448.1 59.7 reduce-scatter.10
  514.1 237.2 all-reduce.4
